TPU v7x, 512 devices: a whole 4x8x8 slice. The times are simulated.
512 devices in a mesh: ctx: 64 (over y, z), tp: 8 (over x, core).
Axes of the slice: x: 4, y: 8, z: 8, core: 2. Of those that a mesh axis runs over, the one named last changes fastest.
Arguments:
- inputs: bfloat16 [8192, 4096], P('ctx', 'tp'), may hold values from -6 to 6
- gate_in: bfloat16 [8192, 4096], P('ctx', 'tp'), may hold values from -6 to 6
- b_proj: bfloat16 [8192, 128], P('ctx'), may hold values from -0.5 to 0.5
- c_proj: bfloat16 [8192, 128], P('ctx'), may hold values from -0.5 to 0.5
- log_decay: float32 [32, 8192], P('tp', 'ctx'), may hold values from -0.75 to 0
- w_out: bfloat16 [4096, 4096], P('tp'), may hold values from -0.09375 to 0.09375
- cotangent: bfloat16 [8192, 4096], P(('ctx', 'tp')), may hold values from -6 to 6
Outputs:
- layer_out: bfloat16 [8192, 4096], P(('ctx', 'tp'))
- grad_inputs: bfloat16 [8192, 4096], P('ctx', 'tp')
- grad_gate: bfloat16 [8192, 4096], P('ctx', 'tp')
- grad_b: float32 [8192, 128], P(('ctx', 'tp'))
- grad_c: float32 [8192, 128], P(('ctx', 'tp'))
- grad_decay: float32 [32, 8192], P('tp', 'ctx')
All inputs are finite; a program needn't handle non-finite values.
Results may differ from a plain program's by a relative error of at most 0.017.
Values may be sent and summed in bfloat16 or wider, within the bound.
No kernel may reach another device: no remote copies, remote signals or barrier semaphores. Data moves between devices by JAX's collectives and lax.ppermute only.
A program may use at most 128 MiB of HBM per device.

v0:
```python
import jax
import jax.numpy as jnp
from jax import lax
from jax.sharding import PartitionSpec as P

BLOCK = 128


def entering(shard, axis, combine, identity, reverse):
    count, place = (lax.axis_size(axis), lax.axis_index(axis))
    everything = jax.tree.map(lambda part: lax.all_gather(part, axis), shard)
    start = jax.tree.map(
        lambda part, zero: jnp.broadcast_to(jnp.asarray(zero, part.dtype), part.shape),
        shard,
        identity,
    )

    def lap(k, before):
        at = count - 1 - k if reverse else k
        reached = at > place if reverse else at < place
        new = combine(before, jax.tree.map(lambda part: part[at], everything))
        return jax.tree.map(lambda a, b: jnp.where(reached, a, b), new, before)

    return lax.fori_loop(0, count, lap, start)


def compose(earlier, later_part):
    return (earlier[0] * later_part[0], later_part[0][:, None, None] * earlier[1] + later_part[1])


def carried(block_decay, block_terms, backward):
    if backward:
        block_decay = jnp.flip(block_decay, 0)
        block_terms = jnp.flip(block_terms, 0)
    head_count = block_decay.shape[1]

    def local_step(running, packed):
        state_level, product = running
        decay_step, term_block = packed
        return (
            (decay_step[:, None, None] * state_level + term_block, decay_step * product),
            (state_level, product),
        )

    initial = (jnp.zeros(block_terms.shape[1:], jnp.float32), jnp.ones((head_count,), jnp.float32))
    (dev_state, dev_decay), (local_in, decay_before) = lax.scan(
        local_step, initial, (block_decay, block_terms)
    )
    identity = (jnp.ones((head_count,), jnp.float32), jnp.zeros(block_terms.shape[1:], jnp.float32))
    if backward:
        incoming = entering((dev_decay, dev_state), "ctx", compose, identity, True)[1]
    else:
        incoming = entering((dev_decay, dev_state), "ctx", compose, identity, False)[1]

    def resume(state_level, packed):
        decay_step, term_block = packed
        return (decay_step[:, None, None] * state_level + term_block, state_level)

    unused, states = lax.scan(resume, incoming, (block_decay, block_terms))
    if backward:
        states = jnp.flip(states, 0)
    return states


def local(inputs, gate_in, b_proj, c_proj, log_decay, w_out, cotangent):
    tok_rows, feature_width = inputs.shape
    head_count = log_decay.shape[0]
    head_dim = feature_width // head_count
    nblocks = tok_rows // BLOCK
    nstate = b_proj.shape[1]
    x_blocks = inputs.reshape(nblocks, BLOCK, head_count, head_dim)
    b_blocks = b_proj.reshape(nblocks, BLOCK, nstate)
    c_blocks = c_proj.reshape(nblocks, BLOCK, nstate)
    d_blocks = jnp.transpose(log_decay.reshape(head_count, nblocks, BLOCK), (1, 2, 0))
    gate_float = gate_in.astype(jnp.float32).reshape(nblocks, BLOCK, head_count, head_dim)
    sigmoid_z = jax.nn.sigmoid(gate_float)
    silu_z = gate_float * sigmoid_z
    position = jnp.arange(BLOCK)
    causal = position[:, None] >= position[None, :]
    lower_ones = causal.astype(jnp.float32)
    cumulative = jnp.einsum("qs,csh->cqh", lower_ones, d_blocks, precision=lax.Precision.HIGHEST)
    final_sum = cumulative[:, -1, :]
    block_decay = jnp.exp(final_sum)
    tail_weight = jnp.exp(final_sum[:, None, :] - cumulative)
    exp_cum = jnp.exp(cumulative)
    column_cum = jnp.transpose(cumulative, (0, 2, 1))
    differ = column_cum[:, :, :, None] - column_cum[:, :, None, :]
    decay_mat = jnp.where(causal, jnp.exp(jnp.minimum(differ, 0.0)), 0.0)
    scores = jnp.einsum("cqn,ckn->cqk", c_blocks, b_blocks, preferred_element_type=jnp.float32)
    mixing_b = (scores[:, None] * decay_mat).astype(jnp.bfloat16)
    y_intra = jnp.einsum("chqk,ckhp->cqhp", mixing_b, x_blocks, preferred_element_type=jnp.float32)
    weighted = (x_blocks.astype(jnp.float32) * tail_weight[..., None]).astype(jnp.bfloat16)
    block_state = jnp.einsum(
        "cqhp,cqn->chpn", weighted, b_blocks, preferred_element_type=jnp.float32
    )
    state_in = carried(block_decay, block_state, False)
    state_b = state_in.astype(jnp.bfloat16)
    y_inter = (
        jnp.einsum("cqn,chpn->cqhp", c_blocks, state_b, preferred_element_type=jnp.float32)
        * exp_cum[..., None]
    )
    y_full = y_intra + y_inter
    gated_out = (y_full * silu_z).astype(jnp.bfloat16).reshape(tok_rows, feature_width)
    layer_out = lax.psum_scatter(
        jnp.dot(gated_out, w_out, preferred_element_type=jnp.float32).astype(jnp.bfloat16),
        "tp",
        scatter_dimension=0,
        tiled=True,
    )
    state_in, state_b, y_inter, y_full, layer_out = (state_in, state_b, y_inter, y_full, layer_out)
    dgated = lax.dot_general(
        lax.all_gather(cotangent, "tp", axis=0, tiled=True),
        w_out,
        (((1,), (1,)), ((), ())),
        preferred_element_type=jnp.float32,
    )
    dgated = dgated.reshape(nblocks, BLOCK, head_count, head_dim)
    grad_y = dgated * silu_z
    grad_w = (grad_y * exp_cum[..., None]).astype(jnp.bfloat16)
    injected = jnp.einsum("cqhp,cqn->chpn", grad_w, c_blocks, preferred_element_type=jnp.float32)
    adjoint_next = carried(block_decay, injected, True)
    dgated, grad_y, grad_w, adjoint_next = (dgated, grad_y, grad_w, adjoint_next)
    grad_gate = (dgated * y_full * (sigmoid_z + gate_float * sigmoid_z * (1.0 - sigmoid_z))).astype(
        jnp.bfloat16
    )
    grad_gate = grad_gate.reshape(tok_rows, feature_width)
    grad_y_b = grad_y.astype(jnp.bfloat16)
    adjoint_b = adjoint_next.astype(jnp.bfloat16)
    pair_dots = jnp.einsum(
        "cqhp,ckhp->chqk", grad_y_b, x_blocks, preferred_element_type=jnp.float32
    )
    dmix = pair_dots * decay_mat
    dmix_b = dmix.astype(jnp.bfloat16)
    state_dx = (
        jnp.einsum("ckn,chpn->ckhp", b_blocks, adjoint_b, preferred_element_type=jnp.float32)
        * tail_weight[..., None]
    )
    grad_inputs = (
        jnp.einsum("chqk,cqhp->ckhp", mixing_b, grad_y_b, preferred_element_type=jnp.float32)
        + state_dx
    )
    grad_inputs = grad_inputs.astype(jnp.bfloat16).reshape(tok_rows, feature_width)
    b_terms = jnp.einsum("chqk,cqn->ckn", dmix_b, c_blocks, preferred_element_type=jnp.float32)
    b_terms = b_terms + jnp.einsum(
        "ckhp,chpn->ckn", weighted, adjoint_b, preferred_element_type=jnp.float32
    )
    c_terms = jnp.einsum("chqk,ckn->cqn", dmix_b, b_blocks, preferred_element_type=jnp.float32)
    c_terms = c_terms + jnp.einsum(
        "cqhp,chpn->cqn", grad_w, state_b, preferred_element_type=jnp.float32
    )
    grad_b, grad_c = (
        lax.psum_scatter(
            b_terms.reshape(tok_rows, nstate).astype(jnp.bfloat16),
            "tp",
            scatter_dimension=0,
            tiled=True,
        ).astype(jnp.float32),
        lax.psum_scatter(
            c_terms.reshape(tok_rows, nstate).astype(jnp.bfloat16),
            "tp",
            scatter_dimension=0,
            tiled=True,
        ).astype(jnp.float32),
    )
    cross_terms = dmix * scores[:, None]
    decay_flow = jnp.transpose(jnp.sum(cross_terms, 3) - jnp.sum(cross_terms, 2), (0, 2, 1))
    outflow = jnp.sum(x_blocks.astype(jnp.float32) * state_dx, 3)
    decay_flow = decay_flow + jnp.sum(grad_y * y_inter, 3) - outflow
    closing = jnp.sum(outflow, 1) + block_decay * jnp.sum(adjoint_next * state_in, (2, 3))
    decay_flow = decay_flow.at[:, -1, :].add(closing)
    grad_decay = jnp.einsum("ut,cuh->cth", lower_ones, decay_flow, precision=lax.Precision.HIGHEST)
    grad_decay = jnp.transpose(grad_decay, (2, 0, 1)).reshape(head_count, tok_rows)
    return (layer_out, grad_inputs, grad_gate, grad_b, grad_c, grad_decay)


def solution(mesh):
    in_specs = (
        P("ctx", "tp"),
        P("ctx", "tp"),
        P("ctx", None),
        P("ctx", None),
        P("tp", "ctx"),
        P("tp", None),
        P(("ctx", "tp"), None),
    )
    out_specs = (
        P(("ctx", "tp"), None),
        P("ctx", "tp"),
        P("ctx", "tp"),
        P(("ctx", "tp"), None),
        P(("ctx", "tp"), None),
        P("tp", "ctx"),
    )
    return jax.shard_map(local, mesh=mesh, in_specs=in_specs, out_specs=out_specs, check_vma=False)
```

profile of v0, /device:TPU:8, one launch (start us, length us, event | category | flops | bytes accessed | tf_op | source)
XLA Modules:
  0.0 479.4 jit_solution(16107612873647827048)
XLA Ops:
  9.3 1.8 convolution_add_fusion.1
  11.4 32.1 %all-gather.7.cloned.1.call-done = bf16[128,4096]{1,0:T(8,128)(2,1)} async-done(((bf16[16,4096]{1,0:T(8,128)(2,1)}), bf16[128,4096]{1,0:T(8,128)(2,1)}) %all-gather.7.cloned.1.call-update) | async-done | bytes 1048592 | tf_op jit(solution)/shard_map/all_gather | solution.py:112
  43.5 4.0 fusion.39
  49.0 45.2 %all-gather = f32[64,1,4]{2,1,0:T(1,128)S(1)} all-gather(f32[1,1,4]{2,1,0:T(1,128)S(1)} %copy.53), channel_id=2, replica_groups=mesh['ctx'=64,'tp'=8] {'ctx'}, dimensions={0}, use_global_device_ids=true | all-gather | bytes 1040 | tf_op jit(solution)/shard_map/all_gather | solution.py:11
  95.1 91.4 %all-gather.9.cloned.1.call-done = f32[256,128,128]{2,1,0:T(8,128)} async-done(((f32[4,128,128]{2,1,0:T(8,128)}), f32[256,128,128]{2,1,0:T(8,128)}) %all-gather.9.cloned.1.call-update) | async-done | bytes 16777232 | tf_op jit(solution)/shard_map/all_gather | solution.py:11
  186.5 70.2 %while.21 = (s32[]{:T(128)}, f32[4,128,128]{2,1,0:T(8,128)S(1)}, s32[]{:T(128)}, f32[64,4]{1,0:T(8,128)S(1)}, f32[64,4,128,128]{3,2,1,0:T(8,128)}, /*index=5*/s32[]{:T(128)}, s32[]{:T(128)}) while((s32[]{:T(128)}, f32[4,128,128]{2,1,0:T(8,128)S(1)}, s32[]{:T(128)}, f32[64,4]{1,0:T(8,128)S(1)}, f32[64,4,128,128]{3,2,1,0:T(8,128)}, ...), condition=%wide.region_1.2_spmd.clone, body=%wide.region_0.1_spmd.clone.sunk | while | flops 262148 | bytes 786585 | solution.py:24
  201.8 1.1 fusion.59
  202.9 1.1 fusion.59
  210.5 1.1 fusion.59
  214.9 1.1 fusion.59
  217.1 1.1 fusion.59
  221.5 1.1 fusion.59
  224.8 1.1 fusion.59
  229.2 1.1 fusion.59
  243.4 1.1 fusion.59
  244.6 1.1 fusion.59
  252.3 1.1 fusion.59
  254.5 1.1 fusion.59
  255.6 1.1 fusion.59
  258.2 69.4 %all-gather.11.cloned.1.call-done = f32[256,128,128]{2,1,0:T(8,128)} async-done(((f32[4,128,128]{2,1,0:T(8,128)}), f32[256,128,128]{2,1,0:T(8,128)}) %all-gather.11.cloned.1.call-update) | async-done | bytes 16777232 | tf_op jit(solution)/shard_map/all_gather | solution.py:11
  327.6 70.8 %while.22 = (s32[]{:T(128)}, f32[4,128,128]{2,1,0:T(8,128)S(1)}, s32[]{:T(128)}, f32[64,4]{1,0:T(8,128)S(1)}, f32[64,4,128,128]{3,2,1,0:T(8,128)}, /*index=5*/s32[]{:T(128)}, s32[]{:T(128)}, s32[]{:T(128)}, s32[]{:T(128)}) while((s32[]{:T(128)}, f32[4,128,128]{2,1,0:T(8,128)S(1)}, s32[]{:T(128)}, f32[64,4]{1,0:T(8,128)S(1)}, ...), condition=%wide.region_4.5_spmd.clone, body=%wide.region_3.4_spmd.clone.sunk | while | flops 262152 | bytes 786647 | solution.py:24
  328.8 1.1 fusion.60
  329.9 1.1 fusion.60
  331.0 1.1 fusion.60
  332.1 1.1 fusion.60
  333.2 1.1 fusion.60
  334.3 1.1 fusion.60
  335.4 1.1 fusion.60
  336.5 1.1 fusion.60
  337.6 1.1 fusion.60
  338.7 1.1 fusion.60
  339.8 1.1 fusion.60
  340.9 1.1 fusion.60
  342.0 1.1 fusion.60
  343.2 1.1 fusion.60
  344.3 1.1 fusion.60
  345.4 1.1 fusion.60
  346.5 1.1 fusion.60
  347.6 1.1 fusion.60
  348.7 1.1 fusion.60
  349.8 1.1 fusion.60
  350.9 1.1 fusion.60
  352.0 1.1 fusion.60
  353.1 1.1 fusion.60
  354.2 1.1 fusion.60
  355.3 1.1 fusion.60
  356.5 1.1 fusion.60
  357.6 1.1 fusion.60
  358.7 1.1 fusion.60
  359.8 1.1 fusion.60
  360.9 1.1 fusion.60
  362.0 1.1 fusion.60
  363.1 1.1 fusion.60
  364.2 1.1 fusion.60
  369.8 1.1 fusion.60
  375.3 1.1 fusion.60
  383.0 1.1 fusion.60
  390.8 1.1 fusion.60
  396.3 1.1 fusion.60
  399.5 3.9 convolution_convert_fusion
  404.3 1.3 convert_element_type.112
  408.2 25.1 %reduce-scatter.6.cloned.1.call-done = bf16[16,128]{1,0:T(8,128)(2,1)} async-done(((bf16[128,128]{1,0:T(8,128)(2,1)}), bf16[16,128]{1,0:T(8,128)(2,1)}) %reduce-scatter.6.cloned.1.call-update) | async-done | bytes 4112 | tf_op jit(solution)/shard_map/reduce_scatter | solution.py:152
  433.3 1.3 convert_element_type.110
  434.5 38.0 %reduce-scatter.4.cloned.1.call-done = bf16[16,4096]{1,0:T(8,128)(2,1)} async-done(((bf16[128,4096]{1,0:T(8,128)(2,1)}), bf16[16,4096]{1,0:T(8,128)(2,1)}) %reduce-scatter.4.cloned.1.call-update) | async-done | bytes 131088 | tf_op jit(solution)/shard_map/reduce_scatter | solution.py:104
  (264 shorter events, 92.8 us)
Async XLA Ops:
  7.2 2.1 copy-start
  7.2 40.3 %copy-start.2 = (bf16[128,512]{1,0:T(8,128)(2,1)S(1)}, bf16[128,512]{1,0:T(8,128)(2,1)}, u32[]{:S(2)}) copy-start(bf16[128,512]{1,0:T(8,128)(2,1)} %param.14) | copy-start | bytes 393220
  7.2 36.3 %all-gather.7.cloned.1.call-start = ((), (), s32[]{:S(2)}) async-start(), calls=%async_computation.4 | async-start | bytes 1179648 | tf_op jit(solution)/shard_map/all_gather | solution.py:112
  7.9 178.5 %all-gather.9.cloned.1.call-start = ((), (), s32[]{:S(2)}) async-start(), calls=%async_computation.7 | async-start | bytes 17039360 | tf_op jit(solution)/shard_map/all_gather | solution.py:11
  9.1 38.5 %copy-start.3 = (bf16[128,128]{1,0:T(8,128)(2,1)S(1)}, bf16[128,128]{1,0:T(8,128)(2,1)}, u32[]{:S(2)}) copy-start(bf16[128,128]{1,0:T(8,128)(2,1)} %param.16) | copy-start | bytes 98308
  11.1 37.5 %copy-start.1 = (bf16[128,512]{1,0:T(8,128)(2,1)S(1)}, bf16[128,512]{1,0:T(8,128)(2,1)}, u32[]{:S(2)}) copy-start(bf16[128,512]{1,0:T(8,128)(2,1)} %param.13) | copy-start | bytes 393220
  11.2 316.5 %all-gather.11.cloned.1.call-start = ((), (), s32[]{:S(2)}) async-start(), calls=%async_computation.8 | async-start | bytes 17039360 | tf_op jit(solution)/shard_map/all_gather | solution.py:11
  48.6 355.7 %reduce-scatter.8.cloned.1.call-start = ((), (), s32[]{:S(2)}) async-start(), calls=%async_computation.6 | async-start | bytes 36864 | tf_op jit(solution)/shard_map/reduce_scatter | solution.py:158
  257.8 175.4 %reduce-scatter.6.cloned.1.call-start = ((), (), s32[]{:S(2)}) async-start(), calls=%async_computation.5 | async-start | bytes 36864 | tf_op jit(solution)/shard_map/reduce_scatter | solution.py:152
  399.5 73.1 %reduce-scatter.4.cloned.1.call-start = ((), (), s32[]{:S(2)}) async-start(), calls=%async_computation.3 | async-start | bytes 1179648 | tf_op jit(solution)/shard_map/reduce_scatter | solution.py:104
Sparse Core Ops, SparseCore 0:
  10.2 33.2 all-gather.6
  46.5 139.9 all-gather.8
  189.5 138.1 all-gather.10
  330.9 33.6 reduce-scatter.7
  399.6 33.5 reduce-scatter.5
  436.5 36.0 reduce-scatter.3
where the time goes:
time: 484 us; the launch traced here: 479 us
  waiting for transfers between devices  257 us (53%)
  other arithmetic  138 us (29%)
  blocking collectives  45.2 us (9%)
  matrix products  15.8 us (3%)
  between operations  14.3 us (3%)
    all_gather x2, waiting for transfers between devices, entering(): everything = jax.tree.map(lambda part: lax.all_gather(part, axis), shard)  161 us
    select_n x128, other arithmetic, lap(): return jax.tree.map(lambda a, b: jnp.where(reached, a, b), new, before)  135 us
    all_gather x1, blocking collectives, entering(): everything = jax.tree.map(lambda part: lax.all_gather(part, axis), shard)  45.2 us
    reduce_scatter x1, waiting for transfers between devices, local(): lax.psum_scatter(jnp.dot(gated_out, w_out, preferred_element_type=jnp.flo...  38 us
    all_gather x1, waiting for transfers between devices, local(): lax.all_gather(cotangent, 'tp', axis=0, tiled=True)  32.1 us
    reduce_scatter x1, waiting for transfers between devices, local(): lax.psum_scatter(b_terms.reshape(tok_rows, nstate).astype(jnp.bfloat16),...  25.1 us
  transfers between devices with their start and end apart: 6, of which 5 were waited for; matrix products, arithmetic and copies ran while one was open for 33% of the time, Pallas kernels for 0%

commit v1 on v0

--- a/solution.py
+++ b/solution.py
@@ -63,6 +63,12 @@
 
 
 def local(inputs, gate_in, b_proj, c_proj, log_decay, w_out, cotangent):
+
+    def target_unite(unit):
+        group_axis = "tp"
+        local_out = jnp.concatenate([unit for _ in range(jax.lax.axis_size(group_axis))], 0)
+        return jax.lax.all_to_all(local_out, group_axis, 0, 0, tiled=True)
+
     tok_rows, feature_width = inputs.shape
     head_count = log_decay.shape[0]
     head_dim = feature_width // head_count
@@ -109,10 +115,7 @@
     )
     state_in, state_b, y_inter, y_full, layer_out = (state_in, state_b, y_inter, y_full, layer_out)
     dgated = lax.dot_general(
-        lax.all_gather(cotangent, "tp", axis=0, tiled=True),
-        w_out,
-        (((1,), (1,)), ((), ())),
-        preferred_element_type=jnp.float32,
+        target_unite(cotangent), w_out, (((1,), (1,)), ((), ())), preferred_element_type=jnp.float32
     )
     dgated = dgated.reshape(nblocks, BLOCK, head_count, head_dim)
     grad_y = dgated * silu_z

time: 484 us -> 453 us (0.936)
  waiting for transfers between devices: 257 us -> 206 us
  local copies, waits for them, and re-layouts: 4.27 us -> 16.8 us
    all_gather x2, waiting for transfers between devices: 161 us -> 127 us  [entering(): everything = jax.tree.map(lambda part: lax.all_gather(part, axis), shard)]
    all_gather x1 -> x0, waiting for transfers between devices: 32.1 us -> none  [local(): lax.all_gather(cotangent, 'tp', axis=0, tiled=True)]
    all_to_all x0 -> x1, waiting for transfers between devices: none -> 15.7 us  [target_unite(): return jax.lax.all_to_all(local_out, group_axis, 0, 0, tiled=True)]
    unnamed x12 -> x19, local copies, waits for them, and re-layouts: 1.78 us -> 12.7 us
  transfers between devices with their start and end apart: 6 -> 6, of which waited for: 5 -> 5; matrix products, arithmetic and copies ran while one was open for 33% -> 37% of each run, Pallas kernels for 0% -> 0%
where the time goes in v1:
time: 453 us; the launch traced here: 448 us
  waiting for transfers between devices  206 us (45%)
  other arithmetic  138 us (30%)
  blocking collectives  48.8 us (11%)
  local copies, waits for them, and re-layouts  16.8 us (4%)
  matrix products  15.6 us (3%)
  between operations  14 us (3%)
  starting transfers between devices  4.64 us (1%)
    select_n x128, other arithmetic, lap(): return jax.tree.map(lambda a, b: jnp.where(reached, a, b), new, before)  135 us
    all_gather x2, waiting for transfers between devices, entering(): everything = jax.tree.map(lambda part: lax.all_gather(part, axis), shard)  127 us
    all_gather x1, blocking collectives, entering(): everything = jax.tree.map(lambda part: lax.all_gather(part, axis), shard)  48.8 us
    reduce_scatter x1, waiting for transfers between devices, local(): lax.psum_scatter(jnp.dot(gated_out, w_out, preferred_element_type=jnp.flo...  38.1 us
    reduce_scatter x1, waiting for transfers between devices, local(): lax.psum_scatter(b_terms.reshape(tok_rows, nstate).astype(jnp.bfloat16),...  25 us
    all_to_all x1, waiting for transfers between devices, target_unite(): return jax.lax.all_to_all(local_out, group_axis, 0, 0, tiled=True)  15.7 us
    unnamed x19, local copies, waits for them, and re-layouts  12.7 us
  transfers between devices with their start and end apart: 6, of which 5 were waited for; matrix products, arithmetic and copies ran while one was open for 37% of the time, Pallas kernels for 0%

profile of v1, /device:TPU:8, one launch (start us, length us, event | category | flops | bytes accessed | tf_op | source)
XLA Modules:
  0.0 448.3 jit_solution(10421244442179180765)
XLA Ops:
  8.5 1.8 convolution_add_fusion.1
  10.4 1.6 constant_dynamic-update-slice_fusion.7
  12.0 1.6 constant_dynamic-update-slice_fusion.6
  13.5 1.6 constant_dynamic-update-slice_fusion.5
  15.1 1.6 constant_dynamic-update-slice_fusion.4
  16.7 1.6 constant_dynamic-update-slice_fusion.3
  18.2 1.6 constant_dynamic-update-slice_fusion.2
  19.8 1.6 constant_dynamic-update-slice_fusion.1
  21.3 1.6 constant_dynamic-update-slice_fusion
  22.9 4.4 all-to-all-start
  27.6 15.7 %all-to-all-done = bf16[8,16,4096]{2,1,0:T(8,128)(2,1)S(1)} async-done(((bf16[8,16,4096]{2,1,0:T(8,128)(2,1)}), bf16[8,16,4096]{2,1,0:T(8,128)(2,1)S(1)}, u32[]{:S(2)}, u32[]{:S(2)}) %all-to-all-start) | async-done | bytes 1048608 | tf_op jit(solution)/shard_map/all_to_all | solution.py:70
  43.3 3.8 fusion.39
  48.6 48.8 %all-gather = f32[64,1,4]{2,1,0:T(1,128)S(1)} all-gather(f32[1,1,4]{2,1,0:T(1,128)S(1)} %copy.53), channel_id=2, replica_groups=mesh['ctx'=64,'tp'=8] {'ctx'}, dimensions={0}, use_global_device_ids=true | all-gather | bytes 1040 | tf_op jit(solution)/shard_map/all_gather | solution.py:11
  98.2 58.0 %all-gather.6.cloned.1.call-done = f32[256,128,128]{2,1,0:T(8,128)} async-done(((f32[4,128,128]{2,1,0:T(8,128)}), f32[256,128,128]{2,1,0:T(8,128)}) %all-gather.6.cloned.1.call-update) | async-done | bytes 16777232 | tf_op jit(solution)/shard_map/all_gather | solution.py:11
  156.2 70.4 %while.21 = (s32[]{:T(128)}, f32[4,128,128]{2,1,0:T(8,128)S(1)}, s32[]{:T(128)}, f32[64,4]{1,0:T(8,128)S(1)}, f32[64,4,128,128]{3,2,1,0:T(8,128)}, /*index=5*/s32[]{:T(128)}, s32[]{:T(128)}) while((s32[]{:T(128)}, f32[4,128,128]{2,1,0:T(8,128)S(1)}, s32[]{:T(128)}, f32[64,4]{1,0:T(8,128)S(1)}, f32[64,4,128,128]{3,2,1,0:T(8,128)}, ...), condition=%wide.region_1.2_spmd.clone, body=%wide.region_0.1_spmd.clone.sunk | while | flops 262148 | bytes 786593 | solution.py:24
  159.5 1.1 fusion.59
  160.6 1.1 fusion.59
  161.7 1.1 fusion.59
  162.8 1.1 fusion.59
  163.9 1.1 fusion.59
  165.0 1.1 fusion.59
  166.1 1.1 fusion.59
  167.2 1.1 fusion.59
  168.3 1.1 fusion.59
  169.4 1.1 fusion.59
  170.5 1.1 fusion.59
  171.6 1.1 fusion.59
  172.7 1.1 fusion.59
  174.9 1.1 fusion.59
  176.0 1.1 fusion.59
  177.1 1.1 fusion.59
  178.2 1.1 fusion.59
  179.3 1.1 fusion.59
  182.6 1.1 fusion.59
  183.7 1.1 fusion.59
  184.8 1.1 fusion.59
  187.0 1.1 fusion.59
  191.4 1.1 fusion.59
  194.7 1.1 fusion.59
  198.0 1.1 fusion.59
  199.1 1.1 fusion.59
  213.4 1.1 fusion.59
  221.1 1.1 fusion.59
  222.3 1.1 fusion.59
  224.5 1.1 fusion.59
  228.2 68.9 %all-gather.8.cloned.1.call-done = f32[256,128,128]{2,1,0:T(8,128)} async-done(((f32[4,128,128]{2,1,0:T(8,128)}), f32[256,128,128]{2,1,0:T(8,128)}) %all-gather.8.cloned.1.call-update) | async-done | bytes 16777232 | tf_op jit(solution)/shard_map/all_gather | solution.py:11
  297.1 70.6 %while.22 = (s32[]{:T(128)}, f32[4,128,128]{2,1,0:T(8,128)S(1)}, s32[]{:T(128)}, f32[64,4]{1,0:T(8,128)S(1)}, f32[64,4,128,128]{3,2,1,0:T(8,128)}, /*index=5*/s32[]{:T(128)}, s32[]{:T(128)}, s32[]{:T(128)}, s32[]{:T(128)}) while((s32[]{:T(128)}, f32[4,128,128]{2,1,0:T(8,128)S(1)}, s32[]{:T(128)}, f32[64,4]{1,0:T(8,128)S(1)}, ...), condition=%wide.region_4.5_spmd.clone, body=%wide.region_3.4_spmd.clone.sunk | while | flops 262152 | bytes 786655 | solution.py:24
  312.5 1.1 fusion.60
  315.9 1.1 fusion.60
  317.0 1.1 fusion.60
  318.1 1.1 fusion.60
  319.2 1.1 fusion.60
  321.4 1.1 fusion.60
  322.5 1.1 fusion.60
  323.6 1.1 fusion.60
  324.7 1.1 fusion.60
  328.0 1.1 fusion.60
  329.1 1.1 fusion.60
  333.5 1.1 fusion.60
  368.8 3.9 convolution_convert_fusion
  373.5 1.3 convert_element_type.112
  377.4 25.0 %reduce-scatter.6.cloned.1.call-done = bf16[16,128]{1,0:T(8,128)(2,1)} async-done(((bf16[128,128]{1,0:T(8,128)(2,1)}), bf16[16,128]{1,0:T(8,128)(2,1)}) %reduce-scatter.6.cloned.1.call-update) | async-done | bytes 4112 | tf_op jit(solution)/shard_map/reduce_scatter | solution.py:155
  402.4 1.3 convert_element_type.110
  403.7 38.1 %reduce-scatter.4.cloned.1.call-done = bf16[16,4096]{1,0:T(8,128)(2,1)} async-done(((bf16[128,4096]{1,0:T(8,128)(2,1)}), bf16[16,4096]{1,0:T(8,128)(2,1)}) %reduce-scatter.4.cloned.1.call-update) | async-done | bytes 131088 | tf_op jit(solution)/shard_map/reduce_scatter | solution.py:110
  (271 shorter events, 101.8 us)
Async XLA Ops:
  7.2 1.4 copy-start
  7.2 149.0 %all-gather.6.cloned.1.call-start = ((), (), s32[]{:S(2)}) async-start(), calls=%async_computation.7 | async-start | bytes 17039360 | tf_op jit(solution)/shard_map/all_gather | solution.py:11
  22.9 24.2 %copy-start.2 = (bf16[128,512]{1,0:T(8,128)(2,1)S(1)}, bf16[128,512]{1,0:T(8,128)(2,1)}, u32[]{:S(2)}) copy-start(bf16[128,512]{1,0:T(8,128)(2,1)} %param.14) | copy-start | bytes 393220
  22.9 24.3 %copy-start.3 = (bf16[128,128]{1,0:T(8,128)(2,1)S(1)}, bf16[128,128]{1,0:T(8,128)(2,1)}, u32[]{:S(2)}) copy-start(bf16[128,128]{1,0:T(8,128)(2,1)} %param.16) | copy-start | bytes 98308
  22.9 20.4 %all-to-all-start = ((bf16[8,16,4096]{2,1,0:T(8,128)(2,1)}), bf16[8,16,4096]{2,1,0:T(8,128)(2,1)S(1)}, u32[]{:S(2)}, u32[]{:S(2)}) async-start(bf16[8,16,4096]{2,1,0:T(8,128)(2,1)} %bitcast.23), calls=%async_computation.1 | async-start | bytes 2097152 | tf_op jit(solution)/shard_map/all_to_all | solution.py:70
  27.3 20.9 %copy-start.1 = (bf16[128,512]{1,0:T(8,128)(2,1)S(1)}, bf16[128,512]{1,0:T(8,128)(2,1)}, u32[]{:S(2)}) copy-start(bf16[128,512]{1,0:T(8,128)(2,1)} %param.13) | copy-start | bytes 393220
  27.4 269.7 %all-gather.8.cloned.1.call-start = ((), (), s32[]{:S(2)}) async-start(), calls=%async_computation.8 | async-start | bytes 17039360 | tf_op jit(solution)/shard_map/all_gather | solution.py:11
  48.2 325.3 %reduce-scatter.8.cloned.1.call-start = ((), (), s32[]{:S(2)}) async-start(), calls=%async_computation.6 | async-start | bytes 36864 | tf_op jit(solution)/shard_map/reduce_scatter | solution.py:161
  227.8 174.6 %reduce-scatter.6.cloned.1.call-start = ((), (), s32[]{:S(2)}) async-start(), calls=%async_computation.5 | async-start | bytes 36864 | tf_op jit(solution)/shard_map/reduce_scatter | solution.py:155
  368.7 73.1 %reduce-scatter.4.cloned.1.call-start = ((), (), s32[]{:S(2)}) async-start(), calls=%async_computation.4 | async-start | bytes 1179648 | tf_op jit(solution)/shard_map/reduce_scatter | solution.py:110
Sparse Core Ops, SparseCore 0:
  11.0 145.1 all-gather.5
  159.2 137.8 all-gather.7
  300.5 33.6 reduce-scatter.7
  368.8 33.5 reduce-scatter.5
  405.7 36.1 reduce-scatter.3
